TPU v7x, 256 devices: a whole 4x4x8 slice. The times are simulated.
256 devices in a mesh: mp: 2 (over x_hi), row: 8 (over z), col: 16 (over x_lo, y, core).
Axes of the slice: x: 4 (x_hi: 2, x_lo: 2; x = x_hi * 2 + x_lo), y: 4, z: 8, core: 2. Of those that a mesh axis runs over, the one named last changes fastest.
Arguments:
- gram_tiles: bfloat16 [4, 16, 8, 128, 16384], P('mp', None, 'row', None, 'col'), may hold values from -4 to 64, as said below
- weights: bfloat16 [4, 16384, 128], P('mp', ('col', 'row')), may hold values from -8 to 8
- damping: float32 [128], replicated, may hold values from 0.5 to 4
Outputs:
- merged: float32 [16384, 128], P(('col', 'row'))
- residual: float32 [16384, 128], P(('col', 'row'))
Inputs may be any that keep to these rules, and one draw needn't show every extreme that they name: `gram_tiles`: each model's 16384 x 16384 Gram, read as in the first step, is symmetric positive definite.
All inputs are finite; a program needn't handle non-finite values.
Results may differ from a plain program's by a relative error of at most 0.012.
The roundings to bfloat16 on the way count: a program that leaves them out, or rounds other values in their place, can miss the bound.
Values may be sent and summed in bfloat16 or wider, within the bound.
No kernel may reach another device: no remote copies, remote signals or barrier semaphores. Data moves between devices by JAX's collectives and lax.ppermute only.
A program may use at most 64 MiB of HBM per device.

v0:
```python
import jax
import jax.numpy as jnp
from jax import lax
from jax.sharding import PartitionSpec as P

ITERS = 2


def contract_rows(gram_tile, portion):
    spread = jnp.broadcast_to(portion, (gram_tile.shape[0],) + portion.shape[1:])
    return jnp.einsum("mij,mjk->ik", gram_tile, spread, preferred_element_type=jnp.float32)


def apply_models(gram_tile, vectors):
    partial_value = contract_rows(gram_tile, lax.all_gather(vectors, "row", axis=1, tiled=True))
    summed = lax.psum_scatter(partial_value, "col", scatter_dimension=0, tiled=True)
    return (lax.psum(summed, "mp"), partial_value)


def squares(residual):
    return lax.psum(jnp.sum(residual * residual, axis=0), ("row", "col"))


def on_device(gram_tiles, weights, damping):
    shape_in = gram_tiles.shape
    gram_tile = gram_tiles.reshape(
        shape_in[0], shape_in[1] * shape_in[2] * shape_in[3], shape_in[4]
    )
    target, unused = apply_models(gram_tile, weights)
    merged = jnp.zeros_like(target)
    residual = target
    direction = target
    norm_now = squares(residual)
    for iteration in range(ITERS):
        low_dir = direction.astype(jnp.bfloat16)
        applied, partial_value = apply_models(gram_tile, low_dir[None])
        dir_wide = low_dir.astype(jnp.float32)
        applied = applied + damping[None, :] * dir_wide
        curve_term = lax.psum(jnp.sum(dir_wide * applied, axis=0), ("row", "col"))
        step_size = norm_now / curve_term
        merged = merged + step_size[None, :] * direction
        residual = residual - step_size[None, :] * applied
        if iteration + 1 < ITERS:
            norm_next = squares(residual)
            direction = residual + (norm_next / norm_now)[None, :] * direction
            norm_now = norm_next
    return (merged, residual)


def solution(mesh):
    in_specs = (P("mp", None, "row", None, "col"), P("mp", ("col", "row"), None), P())
    out_specs = (P(("col", "row"), None), P(("col", "row"), None))
    return jax.shard_map(
        on_device, mesh=mesh, in_specs=in_specs, out_specs=out_specs, check_vma=False
    )
```

profile of v0, /device:TPU:4, one launch (start us, length us, event | category | flops | bytes accessed | tf_op | source)
XLA Modules:
  0.0 1248.6 jit_solution(5157626509282699537)
XLA Ops:
  7.2 0.0 reduce-scatter.4.cloned.1.call-start
  7.2 29.3 %all_gather.9 = bf16[2,1024,128]{2,1,0:T(8,128)(2,1)S(1)} all-gather(bf16[2,128,128]{2,1,0:T(8,128)(2,1)} %param.4), channel_id=1, replica_groups=mesh['mp'=2,'row'=8,'col'=16] {'row'}, dimensions={1}, use_global_device_ids=true | all-gather | bytes 589824 | tf_op jit(solution)/shard_map/all_gather | solution.py:15
  36.5 6.7 convolution_bitcast_fusion.2
  43.3 0.0 reduce-scatter.4.cloned.1.call-update
  43.3 0.0 copy-start.2
  43.3 0.0 all-reduce.5.cloned.1.call-start
  43.3 63.9 %reduce-scatter.4.cloned.1.call-done = f32[128,128]{1,0:T(8,128)} async-done(((f32[2048,128]{1,0:T(8,128)}), f32[128,128]{1,0:T(8,128)}) %reduce-scatter.4.cloned.1.call-update) | async-done | bytes 65552 | tf_op jit(solution)/shard_map/reduce_scatter | solution.py:16
  107.2 0.0 all-reduce.5.cloned.1.call-update
  107.3 0.0 reduce-scatter.6.cloned.1.call-start
  107.3 33.3 %all-reduce.5.cloned.1.call-done = f32[128,128]{1,0:T(8,128)} async-done(((f32[128,128]{1,0:T(8,128)}), f32[128,128]{1,0:T(8,128)}) %all-reduce.5.cloned.1.call-update) | async-done | bytes 65552 | tf_op jit(solution)/shard_map/psum | solution.py:17
  140.6 0.0 copy-start
  140.6 0.9 convert_element_type.12
  141.5 26.0 %all-gather = bf16[1024,128]{1,0:T(8,128)(2,1)S(1)} all-gather(bf16[128,128]{1,0:T(8,128)(2,1)S(1)} %convert_element_type.12), channel_id=2, replica_groups=mesh['mp'=2,'row'=8,'col'=16] {'row'}, dimensions={0}, use_global_device_ids=true | all-gather | bytes 294912 | tf_op jit(solution)/shard_map/all_gather | solution.py:15
  167.6 0.1 copy.5
  167.7 6.7 convolution_bitcast_fusion.1
  174.4 0.0 reduce-scatter.6.cloned.1.call-update
  174.5 0.0 all-reduce.7.cloned.1.call-start
  174.5 65.0 %reduce-scatter.6.cloned.1.call-done = f32[128,128]{1,0:T(8,128)} async-done(((f32[2048,128]{1,0:T(8,128)}), f32[128,128]{1,0:T(8,128)}) %reduce-scatter.6.cloned.1.call-update) | async-done | bytes 65552 | tf_op jit(solution)/shard_map/reduce_scatter | solution.py:16
  239.6 0.0 all-reduce.7.cloned.1.call-update
  239.6 0.0 reduce-scatter.8.cloned.1.call-start
  239.6 33.3 %all-reduce.7.cloned.1.call-done = f32[128,128]{1,0:T(8,128)} async-done(((f32[128,128]{1,0:T(8,128)}), f32[128,128]{1,0:T(8,128)}) %all-reduce.7.cloned.1.call-update) | async-done | bytes 65552 | tf_op jit(solution)/shard_map/psum | solution.py:17
  272.9 0.0 copy-done.2
  272.9 0.0 copy-done
  272.9 0.9 fusion.3
  273.8 0.0 copy-start.1
  273.8 281.3 %all-reduce = (f32[128]{0:T(128)S(1)}, f32[128]{0:T(128)S(1)}) all-reduce(f32[128]{0:T(128)S(1)} %get-tuple-element.3, f32[128]{0:T(128)S(1)} %get-tuple-element.2), channel_id=1, replica_groups=mesh['mp'=2,'row'=8,'col'=16] {'row','col'}, use_global_device_ids=true, to_apply=%region_3.0 | all-reduce | flops 256 | bytes 2048 | tf_op jit(solution)/shard_map/psum | solution.py:21
  555.1 0.9 multiply_reduce_fusion
  556.0 275.6 %psum.53 = f32[128]{0:T(128)S(1)} all-reduce(f32[128]{0:T(128)S(1)} %multiply_reduce_fusion), channel_id=1, replica_groups=mesh['mp'=2,'row'=8,'col'=16] {'row','col'}, use_global_device_ids=true, to_apply=%region_9.0 | all-reduce | flops 128 | bytes 1024 | tf_op jit(solution)/shard_map/psum | solution.py:21
  831.6 0.9 fusion.6
  832.4 24.9 %all-gather.1 = bf16[1024,128]{1,0:T(8,128)(2,1)S(1)} all-gather(bf16[128,128]{1,0:T(8,128)(2,1)S(1)} %fusion.6), channel_id=3, replica_groups=mesh['mp'=2,'row'=8,'col'=16] {'row'}, dimensions={0}, use_global_device_ids=true | all-gather | bytes 294912 | tf_op jit(solution)/shard_map/all_gather | solution.py:15
  857.3 0.1 copy.7
  857.5 6.7 convolution_bitcast_fusion
  864.2 0.0 reduce-scatter.8.cloned.1.call-update
  864.2 0.0 all-reduce.9.cloned.1.call-start
  864.3 60.5 %reduce-scatter.8.cloned.1.call-done = f32[128,128]{1,0:T(8,128)} async-done(((f32[2048,128]{1,0:T(8,128)}), f32[128,128]{1,0:T(8,128)}) %reduce-scatter.8.cloned.1.call-update) | async-done | bytes 65552 | tf_op jit(solution)/shard_map/reduce_scatter | solution.py:16
  924.8 0.0 all-reduce.9.cloned.1.call-update
  924.8 33.2 %all-reduce.9.cloned.1.call-done = f32[128,128]{1,0:T(8,128)} async-done(((f32[128,128]{1,0:T(8,128)}), f32[128,128]{1,0:T(8,128)}) %all-reduce.9.cloned.1.call-update) | async-done | bytes 65552 | tf_op jit(solution)/shard_map/psum | solution.py:17
  958.1 0.9 fusion.5
  958.9 281.3 %psum.55 = f32[128]{0:T(128)S(1)} all-reduce(f32[128]{0:T(128)S(1)} %fusion.5), channel_id=1, replica_groups=mesh['mp'=2,'row'=8,'col'=16] {'row','col'}, use_global_device_ids=true, to_apply=%region_13.0 | all-reduce | flops 128 | bytes 1024 | tf_op jit(solution)/shard_map/psum | solution.py:39
  1240.2 0.0 copy-done.1
  1240.2 1.5 multiply_subtract_fusion
  (3 shorter events, 0.0 us)
Async XLA Ops:
  7.2 100.1 %reduce-scatter.4.cloned.1.call-start = ((), (), s32[]{:S(2)}) async-start(), calls=%async_computation.3 | async-start | bytes 1114112 | tf_op jit(solution)/shard_map/reduce_scatter | solution.py:16
  43.3 229.6 %copy-start.2 = (f32[128]{0:T(128)S(1)}, f32[128]{0:T(128)}, u32[]{:S(2)}) copy-start(f32[128]{0:T(128)} %param.5) | copy-start | bytes 1540
  43.3 97.3 %all-reduce.5.cloned.1.call-start = ((), (), s32[]{:S(2)}) async-start(), calls=%async_computation.4 | async-start | bytes 131072 | tf_op jit(solution)/shard_map/psum | solution.py:17
  107.3 132.3 %reduce-scatter.6.cloned.1.call-start = ((), (), s32[]{:S(2)}) async-start(), calls=%async_computation.5 | async-start | bytes 1114112 | tf_op jit(solution)/shard_map/reduce_scatter | solution.py:16
  140.6 132.3 %copy-start = (f32[128,128]{1,0:T(8,128)S(1)}, f32[128,128]{1,0:T(8,128)}, u32[]{:S(2)}) copy-start(f32[128,128]{1,0:T(8,128)} %all-reduce.5.cloned.1.call-done) | copy-start | bytes 196612
  174.5 98.5 %all-reduce.7.cloned.1.call-start = ((), (), s32[]{:S(2)}) async-start(), calls=%async_computation.6 | async-start | bytes 131072 | tf_op jit(solution)/shard_map/psum | solution.py:17
  239.6 685.2 %reduce-scatter.8.cloned.1.call-start = ((), (), s32[]{:S(2)}) async-start(), calls=%async_computation.7 | async-start | bytes 1114112 | tf_op jit(solution)/shard_map/reduce_scatter | solution.py:16
  273.8 966.4 %copy-start.1 = (f32[128,128]{1,0:T(8,128)S(1)}, f32[128,128]{1,0:T(8,128)}, u32[]{:S(2)}) copy-start(f32[128,128]{1,0:T(8,128)} %all-reduce.7.cloned.1.call-done) | copy-start | bytes 196612
  864.2 93.9 %all-reduce.9.cloned.1.call-start = ((), (), s32[]{:S(2)}) async-start(), calls=%async_computation.8 | async-start | bytes 131072 | tf_op jit(solution)/shard_map/psum | solution.py:17
Sparse Core Ops, SparseCore 0:
  43.4 63.7 reduce-scatter.3
  109.8 30.8 all-reduce.4
  174.6 64.9 reduce-scatter.5
  242.0 30.9 all-reduce.6
  864.3 60.4 reduce-scatter.7
  927.2 30.8 all-reduce.8
where the time goes:
time: 1250 us
  blocking collectives  918 us (73%)
  waiting for transfers between devices  289 us (23%)
  matrix products  20.2 us (2%)
  between operations  14.1 us (1%)
    psum x2, blocking collectives, squares(): return lax.psum(jnp.sum(residual * residual, axis=0), ('row', 'col'))  557 us
    psum x1, blocking collectives, on_device(): curve_term = lax.psum(jnp.sum(dir_wide * applied, axis=0), ('row', 'col'))  281 us
    reduce_scatter x3, waiting for transfers between devices, apply_models(): lax.psum_scatter(partial_value, 'col', scatter_dimension=0, tiled=True)  189 us
    psum x3, waiting for transfers between devices, apply_models(): return (lax.psum(summed, 'mp'), partial_value)  99.9 us
    all_gather x3, blocking collectives, apply_models(): lax.all_gather(vectors, 'row', axis=1, tiled=True)  80.2 us
  transfers between devices with their start and end apart: 6, of which 6 were waited for; matrix products, arithmetic and copies ran while one was open for 0% of the time, Pallas kernels for 0%

commit v1 on v0

--- a/solution.py
+++ b/solution.py
@@ -36,7 +36,7 @@
         applied, partial_value = apply_models(gram_tile, low_dir[None])
         dir_wide = low_dir.astype(jnp.float32)
         applied = applied + damping[None, :] * dir_wide
-        curve_term = lax.psum(jnp.sum(dir_wide * applied, axis=0), ("row", "col"))
+        curve_term = lax.psum(lax.psum(jnp.sum(dir_wide * applied, axis=0), "row"), "col")
         step_size = norm_now / curve_term
         merged = merged + step_size[None, :] * direction
         residual = residual - step_size[None, :] * applied

time: 1250 us -> 1060 us (0.85)
  blocking collectives: 918 us -> 721 us
    psum x1 -> x4, blocking collectives: 281 us -> 88.8 us  [the longest x2 54.3 us: on_device(): lax.psum(lax.psum(jnp.sum(dir_wide * applied, axis=0), 'row'), 'col')]
where the time goes in v1:
time: 1060 us; the launch traced here: 1050 us
  blocking collectives  721 us (68%)
  waiting for transfers between devices  290 us (27%)
  matrix products  20.2 us (2%)
  between operations  14.1 us (1%)
    psum x2, blocking collectives, squares(): return lax.psum(jnp.sum(residual * residual, axis=0), ('row', 'col'))  551 us
    reduce_scatter x3, waiting for transfers between devices, apply_models(): lax.psum_scatter(partial_value, 'col', scatter_dimension=0, tiled=True)  190 us
    psum x3, waiting for transfers between devices, apply_models(): return (lax.psum(summed, 'mp'), partial_value)  99.9 us
    all_gather x3, blocking collectives, apply_models(): lax.all_gather(vectors, 'row', axis=1, tiled=True)  80.2 us
    psum x2, blocking collectives, on_device(): lax.psum(lax.psum(jnp.sum(dir_wide * applied, axis=0), 'row'), 'col')  54.3 us
    psum x2, blocking collectives, on_device(): lax.psum(jnp.sum(dir_wide * applied, axis=0), 'row')  34.5 us
  transfers between devices with their start and end apart: 6, of which 6 were waited for; matrix products, arithmetic and copies ran while one was open for 0% of the time, Pallas kernels for 0%

profile of v1, /device:TPU:4, one launch (start us, length us, event | category | flops | bytes accessed | tf_op | source)
XLA Modules:
  0.0 1051.1 jit_solution(5415844122452989945)
XLA Ops:
  7.2 0.0 reduce-scatter.4.cloned.1.call-start
  7.2 29.3 %all_gather.9 = bf16[2,1024,128]{2,1,0:T(8,128)(2,1)S(1)} all-gather(bf16[2,128,128]{2,1,0:T(8,128)(2,1)} %param.4), channel_id=1, replica_groups=mesh['mp'=2,'row'=8,'col'=16] {'row'}, dimensions={1}, use_global_device_ids=true | all-gather | bytes 589824 | tf_op jit(solution)/shard_map/all_gather | solution.py:15
  36.5 6.7 convolution_bitcast_fusion.2
  43.3 0.0 reduce-scatter.4.cloned.1.call-update
  43.3 0.0 copy-start.2
  43.3 0.0 all-reduce.4.cloned.1.call-start
  43.3 63.9 %reduce-scatter.4.cloned.1.call-done = f32[128,128]{1,0:T(8,128)} async-done(((f32[2048,128]{1,0:T(8,128)}), f32[128,128]{1,0:T(8,128)}) %reduce-scatter.4.cloned.1.call-update) | async-done | bytes 65552 | tf_op jit(solution)/shard_map/reduce_scatter | solution.py:16
  107.2 0.0 all-reduce.4.cloned.1.call-update
  107.3 0.0 reduce-scatter.6.cloned.1.call-start
  107.3 33.3 %all-reduce.4.cloned.1.call-done = f32[128,128]{1,0:T(8,128)} async-done(((f32[128,128]{1,0:T(8,128)}), f32[128,128]{1,0:T(8,128)}) %all-reduce.4.cloned.1.call-update) | async-done | bytes 65552 | tf_op jit(solution)/shard_map/psum | solution.py:17
  140.6 0.0 copy-start
  140.6 0.9 convert_element_type.12
  141.5 26.0 %all-gather = bf16[1024,128]{1,0:T(8,128)(2,1)S(1)} all-gather(bf16[128,128]{1,0:T(8,128)(2,1)S(1)} %convert_element_type.12), channel_id=2, replica_groups=mesh['mp'=2,'row'=8,'col'=16] {'row'}, dimensions={0}, use_global_device_ids=true | all-gather | bytes 294912 | tf_op jit(solution)/shard_map/all_gather | solution.py:15
  167.6 0.1 copy.5
  167.7 6.7 convolution_bitcast_fusion.1
  174.4 0.0 reduce-scatter.6.cloned.1.call-update
  174.5 0.0 all-reduce.6.cloned.1.call-start
  174.5 65.0 %reduce-scatter.6.cloned.1.call-done = f32[128,128]{1,0:T(8,128)} async-done(((f32[2048,128]{1,0:T(8,128)}), f32[128,128]{1,0:T(8,128)}) %reduce-scatter.6.cloned.1.call-update) | async-done | bytes 65552 | tf_op jit(solution)/shard_map/reduce_scatter | solution.py:16
  239.6 0.0 all-reduce.6.cloned.1.call-update
  239.6 0.0 reduce-scatter.8.cloned.1.call-start
  239.6 33.3 %all-reduce.6.cloned.1.call-done = f32[128,128]{1,0:T(8,128)} async-done(((f32[128,128]{1,0:T(8,128)}), f32[128,128]{1,0:T(8,128)}) %all-reduce.6.cloned.1.call-update) | async-done | bytes 65552 | tf_op jit(solution)/shard_map/psum | solution.py:17
  272.9 0.0 copy-done.2
  272.9 0.0 copy-done
  272.9 0.9 fusion.3
  273.8 0.0 copy-start.1
  273.8 17.3 %psum.66 = f32[128]{0:T(128)S(1)} all-reduce(f32[128]{0:T(128)S(1)} %get-tuple-element.2), channel_id=1, replica_groups=mesh['mp'=2,'row'=8,'col'=16] {'row'}, use_global_device_ids=true, to_apply=%region_7.0 | all-reduce | flops 128 | bytes 1024 | tf_op jit(solution)/shard_map/psum | solution.py:39
  291.1 27.2 %psum.67 = f32[128]{0:T(128)S(1)} all-reduce(f32[128]{0:T(128)S(1)} %psum.66), channel_id=1, replica_groups=mesh['mp'=2,'row'=8,'col'=16] {'col'}, use_global_device_ids=true, to_apply=%region_8.0 | all-reduce | flops 128 | bytes 1024 | tf_op jit(solution)/shard_map/psum | solution.py:39
  318.3 275.9 %psum.64 = f32[128]{0:T(128)S(1)} all-reduce(f32[128]{0:T(128)S(1)} %get-tuple-element.3), channel_id=1, replica_groups=mesh['mp'=2,'row'=8,'col'=16] {'row','col'}, use_global_device_ids=true, to_apply=%region_3.0 | all-reduce | flops 128 | bytes 1024 | tf_op jit(solution)/shard_map/psum | solution.py:21
  594.2 0.9 multiply_reduce_fusion
  595.1 275.6 %psum.68 = f32[128]{0:T(128)S(1)} all-reduce(f32[128]{0:T(128)S(1)} %multiply_reduce_fusion), channel_id=1, replica_groups=mesh['mp'=2,'row'=8,'col'=16] {'row','col'}, use_global_device_ids=true, to_apply=%region_10.0 | all-reduce | flops 128 | bytes 1024 | tf_op jit(solution)/shard_map/psum | solution.py:21
  870.7 0.9 fusion.6
  871.5 24.9 %all-gather.1 = bf16[1024,128]{1,0:T(8,128)(2,1)S(1)} all-gather(bf16[128,128]{1,0:T(8,128)(2,1)S(1)} %fusion.6), channel_id=3, replica_groups=mesh['mp'=2,'row'=8,'col'=16] {'row'}, dimensions={0}, use_global_device_ids=true | all-gather | bytes 294912 | tf_op jit(solution)/shard_map/all_gather | solution.py:15
  896.4 0.1 copy.7
  896.6 6.7 convolution_bitcast_fusion
  903.3 0.0 reduce-scatter.8.cloned.1.call-update
  903.3 0.0 all-reduce.8.cloned.1.call-start
  903.4 60.9 %reduce-scatter.8.cloned.1.call-done = f32[128,128]{1,0:T(8,128)} async-done(((f32[2048,128]{1,0:T(8,128)}), f32[128,128]{1,0:T(8,128)}) %reduce-scatter.8.cloned.1.call-update) | async-done | bytes 65552 | tf_op jit(solution)/shard_map/reduce_scatter | solution.py:16
  964.3 0.0 all-reduce.8.cloned.1.call-update
  964.3 33.2 %all-reduce.8.cloned.1.call-done = f32[128,128]{1,0:T(8,128)} async-done(((f32[128,128]{1,0:T(8,128)}), f32[128,128]{1,0:T(8,128)}) %all-reduce.8.cloned.1.call-update) | async-done | bytes 65552 | tf_op jit(solution)/shard_map/psum | solution.py:17
  997.5 0.9 fusion.5
  998.4 17.2 %psum.70 = f32[128]{0:T(128)S(1)} all-reduce(f32[128]{0:T(128)S(1)} %fusion.5), channel_id=1, replica_groups=mesh['mp'=2,'row'=8,'col'=16] {'row'}, use_global_device_ids=true, to_apply=%region_14.0 | all-reduce | flops 128 | bytes 1024 | tf_op jit(solution)/shard_map/psum | solution.py:39
  1015.6 27.2 %psum.71 = f32[128]{0:T(128)S(1)} all-reduce(f32[128]{0:T(128)S(1)} %psum.70), channel_id=1, replica_groups=mesh['mp'=2,'row'=8,'col'=16] {'col'}, use_global_device_ids=true, to_apply=%region_15.0 | all-reduce | flops 128 | bytes 1024 | tf_op jit(solution)/shard_map/psum | solution.py:39
  1042.8 0.0 copy-done.1
  1042.8 1.5 multiply_subtract_fusion
  (3 shorter events, 0.0 us)
Async XLA Ops:
  7.2 100.1 %reduce-scatter.4.cloned.1.call-start = ((), (), s32[]{:S(2)}) async-start(), calls=%async_computation.3 | async-start | bytes 1114112 | tf_op jit(solution)/shard_map/reduce_scatter | solution.py:16
  43.3 229.6 %copy-start.2 = (f32[128]{0:T(128)S(1)}, f32[128]{0:T(128)}, u32[]{:S(2)}) copy-start(f32[128]{0:T(128)} %param.5) | copy-start | bytes 1540
  43.3 97.3 %all-reduce.4.cloned.1.call-start = ((), (), s32[]{:S(2)}) async-start(), calls=%async_computation.4 | async-start | bytes 131072 | tf_op jit(solution)/shard_map/psum | solution.py:17
  107.3 132.3 %reduce-scatter.6.cloned.1.call-start = ((), (), s32[]{:S(2)}) async-start(), calls=%async_computation.5 | async-start | bytes 1114112 | tf_op jit(solution)/shard_map/reduce_scatter | solution.py:16
  140.6 132.3 %copy-start = (f32[128,128]{1,0:T(8,128)S(1)}, f32[128,128]{1,0:T(8,128)}, u32[]{:S(2)}) copy-start(f32[128,128]{1,0:T(8,128)} %all-reduce.4.cloned.1.call-done) | copy-start | bytes 196612
  174.5 98.5 %all-reduce.6.cloned.1.call-start = ((), (), s32[]{:S(2)}) async-start(), calls=%async_computation.6 | async-start | bytes 131072 | tf_op jit(solution)/shard_map/psum | solution.py:17
  239.6 724.7 %reduce-scatter.8.cloned.1.call-start = ((), (), s32[]{:S(2)}) async-start(), calls=%async_computation.7 | async-start | bytes 1114112 | tf_op jit(solution)/shard_map/reduce_scatter | solution.py:16
  273.8 769.0 %copy-start.1 = (f32[128,128]{1,0:T(8,128)S(1)}, f32[128,128]{1,0:T(8,128)}, u32[]{:S(2)}) copy-start(f32[128,128]{1,0:T(8,128)} %all-reduce.6.cloned.1.call-done) | copy-start | bytes 196612
  903.3 94.2 %all-reduce.8.cloned.1.call-start = ((), (), s32[]{:S(2)}) async-start(), calls=%async_computation.8 | async-start | bytes 131072 | tf_op jit(solution)/shard_map/psum | solution.py:17
Sparse Core Ops, SparseCore 0:
  43.4 63.7 reduce-scatter.3
  109.8 30.8 all-reduce.3
  174.6 64.9 reduce-scatter.5
  242.0 30.9 all-reduce.5
  903.4 60.7 reduce-scatter.7
  966.7 30.8 all-reduce.7
